TPU v7x, 32 devices: a whole 2x2x4 slice. The times are simulated.
32 devices in a mesh: parts: 2 (over y), seq: 8 (over z, core), rep: 2 (over x), head: 1.
Axes of the slice: x: 2, y: 2, z: 4, core: 2. Of those that a mesh axis runs over, the one named last changes fastest.
Arguments:
- activations: bfloat16 [4, 1024, 2048], P(('parts', 'rep'), 'seq', 'head'), parts along dimension 0, may hold values from -6 to 6
- value_weight: bfloat16 [2048, 2048], P(('seq', 'rep'), 'head'), may hold values from -0.125 to 0.125
- query_in: bfloat16 [4, 1024, 2048], P(('parts', 'rep'), 'seq', 'head'), parts along dimension 0, may hold values from -6 to 6
- key_in: bfloat16 [4, 1024, 2048], P(('parts', 'rep'), 'seq', 'head'), parts along dimension 0, may hold values from -6 to 6
- grad_out: bfloat16 [4, 1024, 2048], P(('parts', 'rep'), 'seq', 'head'), parts along dimension 0, may hold values from -6 to 6
- conv_kernel: float32 [3, 4, 2048], P(None, None, 'head'), may hold values from -3 to 3
- log_gate: float32 [4, 16, 1024], P(('parts', 'rep'), 'head', 'seq'), parts along dimension 0, as said below
Outputs:
- attn_out: bfloat16 [4, 1024, 2048], P(('parts', 'rep'), 'seq', 'head'), parts along dimension 0
- grad_query: bfloat16 [4, 1024, 2048], P(('parts', 'rep'), 'seq', 'head'), parts along dimension 0
- grad_key: bfloat16 [4, 1024, 2048], P(('parts', 'rep'), 'seq', 'head'), parts along dimension 0
- grad_x: bfloat16 [4, 1024, 2048], P(('parts', 'rep'), 'seq', 'head'), parts along dimension 0
- grad_w: float32 [4096, 2048], P(('parts', 'seq', 'rep'), 'head'), parts along dimension 0
- grad_conv: float32 [6, 4, 2048], P('parts', None, 'head'), parts along dimension 0
There are 2 independent parts, one for each index of `parts`. A program takes and returns all parts, laid end to end along the dimension named above; an argument that names none is the same for every part. Nothing has to cross between parts.
Inputs may be any that keep to these rules, and one draw needn't show every extreme that they name: `log_gate`: every entry is below zero.
All inputs are finite; a program needn't handle non-finite values.
Results may differ from a plain program's by a relative error of at most 0.015.
Values may be sent and summed in bfloat16 or wider, within the bound.
A program may use at most 128 MiB of HBM per device.

v0:
```python
import math
import jax
import jax.numpy as jnp
from jax import lax
from jax.sharding import PartitionSpec as P

EPSILON = 1e-06


def shifted(block, axis, distance):
    devices = range(lax.axis_size(axis))
    route = [(i - distance, i) for i in devices if i - distance in devices]
    return lax.ppermute(block, axis, route)


def prefix(part, axis, combine, identity, reverse):
    count = lax.axis_size(axis)
    place = lax.axis_index(axis)
    ahead = count - 1 - place if reverse else place
    gathered = jax.tree.map(lambda a: lax.all_gather(a, axis), part)
    state = jax.tree.map(lambda a, e: jnp.zeros_like(a) + jnp.asarray(e, a.dtype), part, identity)

    def one(step, state):
        source = count - 1 - step if reverse else step
        return combine(
            state, jax.tree.map(lambda a: lax.dynamic_index_in_dim(a, source, 0, False), gathered)
        )

    return lax.fori_loop(0, ahead, one, state)


def carried_in(value, axis, combine, identity, reverse):
    length, mine = (lax.axis_size(axis), lax.axis_index(axis))
    everything = jax.tree.map(
        lambda part, kind: lax.all_gather(part.astype(kind), axis),
        value,
        (jnp.bfloat16, jnp.bfloat16),
    )
    start = jax.tree.map(
        lambda part, zero: jnp.broadcast_to(jnp.asarray(zero, part.dtype), part.shape),
        value,
        identity,
    )

    def step(k, before):
        at = length - 1 - k if reverse else k
        reached = at > mine if reverse else at < mine
        new = combine(
            before, jax.tree.map(lambda part, own: part[at].astype(own.dtype), everything, value)
        )
        return jax.tree.map(lambda a, b: jnp.where(reached, a, b), new, before)

    return lax.fori_loop(0, length, step, start)


def chain_join(earlier, following):
    return (earlier[0] * following[0], following[0][:, None, None] * earlier[1] + following[1])


def causal_filter(stream_rows, previous, kernel_taps):
    rim_rows = previous.shape[0]
    length = stream_rows.shape[0]
    extended = jnp.concatenate([previous, stream_rows], axis=0).astype(jnp.float32)
    result = jnp.zeros(stream_rows.shape, jnp.float32)
    for offset in range(kernel_taps.shape[0]):
        result = (
            result + kernel_taps[offset] * extended[rim_rows - offset : rim_rows - offset + length]
        )
    return result


def filter_back(post_rows, following_rows, kernel_taps):
    length = post_rows.shape[0]
    extended = jnp.concatenate([post_rows, following_rows], axis=0)
    result = jnp.zeros(post_rows.shape, jnp.float32)
    for offset in range(kernel_taps.shape[0]):
        result = result + kernel_taps[offset] * extended[offset : offset + length]
    return result


def tap_sums(post_rows, stream_rows, previous, kernel_width):
    rim_rows = previous.shape[0]
    length = stream_rows.shape[0]
    extended = jnp.concatenate([previous, stream_rows], axis=0).astype(jnp.float32)
    return jnp.stack(
        [
            jnp.sum(post_rows * extended[rim_rows - offset : rim_rows - offset + length], axis=0)
            for offset in range(kernel_width)
        ]
    )


def local(activations, value_weight, query_in, key_in, grad_out, conv_kernel, log_gate):
    tok_rows = query_in.shape[1]
    channels = query_in.shape[2]
    head_count = log_gate.shape[1]
    head_size = channels // head_count
    kernel_width = conv_kernel.shape[1]
    rim_rows = kernel_width - 1
    grad_scale = 1.0 / math.sqrt(lax.axis_size("seq") * lax.axis_size("rep") * tok_rows)
    query_rows = query_in[0]
    key_rows = key_in[0]
    gathered = lax.all_gather(activations, "head", axis=2, tiled=True)[0]
    columns = gathered
    value_f32 = jnp.dot(
        columns,
        lax.all_gather(value_weight, ("seq", "rep"), axis=0, tiled=True),
        preferred_element_type=jnp.float32,
    )
    value_raw = value_f32.astype(jnp.bfloat16)
    before_all = shifted(
        jnp.stack(
            [
                query_rows[tok_rows - rim_rows :],
                key_rows[tok_rows - rim_rows :],
                value_raw[tok_rows - rim_rows :],
            ]
        ),
        "seq",
        1,
    )
    before = (before_all[0], before_all[1], before_all[2])
    raw_rows = (query_rows, key_rows, value_raw)
    convolved = [
        causal_filter(raw_rows[which], before[which], conv_kernel[which]).astype(jnp.bfloat16)
        for which in range(3)
    ]
    query_heads = convolved[0].reshape(tok_rows, head_count, head_size)
    key_heads = convolved[1].reshape(tok_rows, head_count, head_size)
    value_heads = convolved[2].reshape(tok_rows, head_count, head_size)
    cumulative = jnp.cumsum(log_gate[0], axis=1)
    final_cum = cumulative[:, -1]
    block_decay = jnp.exp(final_cum)
    rising = jnp.exp(cumulative).T[:, :, None]
    shrink = jnp.exp(final_cum[:, None] - cumulative).T[:, :, None]
    mixing = jnp.exp(-jnp.abs(cumulative[:, :, None] - cumulative[:, None, :]))
    scores = (
        mixing
        * jnp.einsum("thd,shd->hts", query_heads, key_heads, preferred_element_type=jnp.float32)
    ).astype(jnp.bfloat16)
    fwd_sum = jnp.einsum(
        "thd,the->hde",
        (shrink * key_heads).astype(jnp.bfloat16),
        value_heads,
        preferred_element_type=jnp.float32,
    )
    back_sum = jnp.einsum(
        "thd,the->hde",
        (rising * key_heads).astype(jnp.bfloat16),
        value_heads,
        preferred_element_type=jnp.float32,
    )
    identity = (
        jnp.ones((head_count,), jnp.float32),
        jnp.zeros((head_count, head_size, head_size), jnp.float32),
    )
    left_b = prefix((block_decay, fwd_sum), "seq", chain_join, identity, False)[1].astype(
        jnp.bfloat16
    )
    right_b = prefix((block_decay, back_sum), "seq", chain_join, identity, True)[1].astype(
        jnp.bfloat16
    )
    attn = rising * jnp.einsum(
        "thd,hde->the", query_heads, left_b, preferred_element_type=jnp.float32
    )
    attn = attn + shrink * jnp.einsum(
        "thd,hde->the", query_heads, right_b, preferred_element_type=jnp.float32
    )
    attn = attn + jnp.einsum(
        "hts,she->the", scores, value_heads, preferred_element_type=jnp.float32
    )
    root_mean = jnp.sqrt(jnp.mean(attn * attn, axis=2, keepdims=True) + EPSILON)
    normed = attn / root_mean
    attn_out = normed.astype(jnp.bfloat16).reshape(1, tok_rows, channels)
    upstream = grad_out[0].reshape(tok_rows, head_count, head_size).astype(jnp.float32)
    grad_attn = (
        (upstream - normed * jnp.mean(upstream * normed, axis=2, keepdims=True)) / root_mean
    ).astype(jnp.bfloat16)
    grad_scores = (
        mixing
        * jnp.einsum("the,she->hts", grad_attn, value_heads, preferred_element_type=jnp.float32)
    ).astype(jnp.bfloat16)
    fwd_grad = jnp.einsum(
        "thd,the->hde",
        (shrink * query_heads).astype(jnp.bfloat16),
        grad_attn,
        preferred_element_type=jnp.float32,
    )
    back_grad = jnp.einsum(
        "thd,the->hde",
        (rising * query_heads).astype(jnp.bfloat16),
        grad_attn,
        preferred_element_type=jnp.float32,
    )
    left_gb = carried_in((block_decay, fwd_grad), "seq", chain_join, identity, False)[1].astype(
        jnp.bfloat16
    )
    right_gb = carried_in((block_decay, back_grad), "seq", chain_join, identity, True)[1].astype(
        jnp.bfloat16
    )
    query_post = rising * jnp.einsum(
        "the,hde->thd", grad_attn, left_b, preferred_element_type=jnp.float32
    )
    query_post = query_post + shrink * jnp.einsum(
        "the,hde->thd", grad_attn, right_b, preferred_element_type=jnp.float32
    )
    query_post = query_post + jnp.einsum(
        "hts,shd->thd", grad_scores, key_heads, preferred_element_type=jnp.float32
    )
    key_post = rising * jnp.einsum(
        "the,hde->thd", value_heads, left_gb, preferred_element_type=jnp.float32
    )
    key_post = key_post + shrink * jnp.einsum(
        "the,hde->thd", value_heads, right_gb, preferred_element_type=jnp.float32
    )
    key_post = key_post + jnp.einsum(
        "hts,thd->shd", grad_scores, query_heads, preferred_element_type=jnp.float32
    )
    value_post = rising * jnp.einsum(
        "thd,hde->the", key_heads, left_gb, preferred_element_type=jnp.float32
    )
    value_post = value_post + shrink * jnp.einsum(
        "thd,hde->the", key_heads, right_gb, preferred_element_type=jnp.float32
    )
    value_post = value_post + jnp.einsum(
        "hts,the->she", scores, grad_attn, preferred_element_type=jnp.float32
    )
    post_grads = jnp.stack(
        [
            query_post.reshape(tok_rows, channels),
            key_post.reshape(tok_rows, channels),
            value_post.reshape(tok_rows, channels),
        ]
    )
    following = shifted(post_grads[:, :rim_rows].astype(jnp.bfloat16), "seq", -1).astype(
        jnp.float32
    )
    grad_query = filter_back(post_grads[0], following[0], conv_kernel[0]).astype(jnp.bfloat16)
    grad_key = filter_back(post_grads[1], following[1], conv_kernel[1]).astype(jnp.bfloat16)
    grad_value = filter_back(post_grads[2], following[2], conv_kernel[2]).astype(jnp.bfloat16)
    kernel_terms = (
        jnp.stack(
            [
                tap_sums(post_grads[which], raw_rows[which], before[which], kernel_width)
                for which in range(3)
            ]
        )
        * grad_scale
    )
    grad_conv = lax.psum(kernel_terms, ("seq", "rep"))
    partial_x = lax.dot_general(
        grad_value,
        lax.all_gather(value_weight, ("seq", "rep"), axis=0, tiled=True),
        (((1,), (1,)), ((), ())),
        preferred_element_type=jnp.float32,
    )
    grad_x = lax.psum_scatter(
        partial_x[None].astype(jnp.bfloat16), "head", scatter_dimension=2, tiled=True
    )
    columns = gathered
    grad_w = lax.psum_scatter(
        lax.dot_general(
            columns, grad_value, (((0,), (0,)), ((), ())), preferred_element_type=jnp.float32
        )
        * grad_scale,
        ("seq", "rep"),
        scatter_dimension=0,
        tiled=True,
    )
    return (attn_out, grad_query[None], grad_key[None], grad_x, grad_w, grad_conv)


def solution(mesh):
    placed = (
        P(("parts", "rep"), "seq", "head"),
        P(("seq", "rep"), "head"),
        P(("parts", "rep"), "seq", "head"),
        P(("parts", "rep"), "seq", "head"),
        P(("parts", "rep"), "seq", "head"),
        P(None, None, "head"),
        P(("parts", "rep"), "head", "seq"),
    )
    return jax.shard_map(
        local,
        mesh=mesh,
        in_specs=placed,
        out_specs=(
            P(("parts", "rep"), "seq", "head"),
            P(("parts", "rep"), "seq", "head"),
            P(("parts", "rep"), "seq", "head"),
            P(("parts", "rep"), "seq", "head"),
            P(("parts", "seq", "rep"), "head"),
            P("parts", None, "head"),
        ),
        check_vma=False,
    )
```

profile of v0, /device:TPU:0, one launch (start us, length us, event | category | flops | bytes accessed | tf_op | source)
XLA Modules:
  0.0 710.2 jit_solution(15877381056896727067)
XLA Ops:
  11.9 75.4 %all-gather.12.cloned.1.call-done = bf16[2048,2048]{1,0:T(8,128)(2,1)} async-done(((bf16[128,2048]{1,0:T(8,128)(2,1)}), bf16[2048,2048]{1,0:T(8,128)(2,1)}) %all-gather.12.cloned.1.call-update) | async-done | bytes 8388624 | tf_op jit(solution)/shard_map/all_gather | solution.py:107
  87.2 4.6 convolution_convert_fusion.1
  105.4 16.3 %all-reduce = f32[128]{0:T(128)S(1)} all-reduce(f32[128]{0:T(128)S(1)} %dynamic-update-slice), channel_id=2, replica_groups=mesh['parts'=2,'seq'=8,'rep'=2,'head'=1] {'seq'}, use_global_device_ids=true, to_apply=%add | all-reduce | flops 128 | bytes 1024
  127.9 54.5 %all-gather.14.cloned.1.call-done = f32[128,128,128]{2,1,0:T(8,128)} async-done(((f32[16,128,128]{2,1,0:T(8,128)}), f32[128,128,128]{2,1,0:T(8,128)}) %all-gather.14.cloned.1.call-update) | async-done | bytes 8388624 | tf_op jit(solution)/shard_map/all_gather | solution.py:20
  186.2 78.5 %all-gather.16.cloned.1.call-done = f32[128,128,128]{2,1,0:T(8,128)} async-done(((f32[16,128,128]{2,1,0:T(8,128)}), f32[128,128,128]{2,1,0:T(8,128)}) %all-gather.16.cloned.1.call-update) | async-done | bytes 8388624 | tf_op jit(solution)/shard_map/all_gather | solution.py:20
  265.8 18.6 %while.57 = (s32[]{:T(128)}, f32[16,128,128]{2,1,0:T(8,128)}, s32[]{:T(128)}, f32[8,16]{1,0:T(8,128)S(1)}, f32[8,16,128,128]{3,2,1,0:T(8,128)}, /*index=5*/s32[]{:T(128)}, s32[]{:T(128)}, s32[]{:T(128)}, s32[]{:T(128)}) while((s32[]{:T(128)}, f32[16,128,128]{2,1,0:T(8,128)}, s32[]{:T(128)}, f32[8,16]{1,0:T(8,128)S(1)}, ...), condition=%wide.region_4.5_spmd, body=%wide.region_3.4_spmd.sunk | while | flops 524294 | bytes 3146075 | solution.py:29
  265.8 2.7 bitcast_add_fusion.5
  268.4 2.7 bitcast_add_fusion.5
  271.1 2.7 bitcast_add_fusion.5
  273.8 2.7 bitcast_add_fusion.5
  276.4 2.7 bitcast_add_fusion.5
  279.1 2.7 bitcast_add_fusion.5
  293.9 14.5 %all-reduce.1 = bf16[128]{0:T(256)(128)(2,1)S(1)} all-reduce(bf16[128]{0:T(256)(128)(2,1)S(1)} %dynamic-update-slice.1), channel_id=7, replica_groups=mesh['parts'=2,'seq'=8,'rep'=2,'head'=1] {'seq'}, use_global_device_ids=true, to_apply=%add.1 | all-reduce | flops 128 | bytes 512
  316.6 19.6 %all-gather.18.cloned.1.call-done = bf16[128,128,128]{2,1,0:T(8,128)(2,1)} async-done(((bf16[16,128,128]{2,1,0:T(8,128)(2,1)}), bf16[128,128,128]{2,1,0:T(8,128)(2,1)}) %all-gather.18.cloned.1.call-update) | async-done | bytes 4194320 | tf_op jit(solution)/shard_map/all_gather | solution.py:35
  336.2 20.2 %while.58 = (s32[]{:T(128)}, f32[16,128,128]{2,1,0:T(8,128)}, s32[]{:T(128)}, bf16[8,16]{1,0:T(8,128)(2,1)S(1)}, bf16[8,16,128,128]{3,2,1,0:T(8,128)(2,1)}, /*index=5*/s32[]{:T(128)}, s32[]{:T(128)}) while((s32[]{:T(128)}, f32[16,128,128]{2,1,0:T(8,128)}, s32[]{:T(128)}, bf16[8,16]{1,0:T(8,128)(2,1)S(1)}, ...), condition=%wide.region_8.9_spmd.clone, body=%wide.region_7.8_spmd.clone.sunk | while | flops 1310740 | bytes 2621713 | solution.py:53
  356.4 2.8 fusion.6
  360.7 22.6 %all-gather.20.cloned.1.call-done = bf16[128,128,128]{2,1,0:T(8,128)(2,1)} async-done(((bf16[16,128,128]{2,1,0:T(8,128)(2,1)}), bf16[128,128,128]{2,1,0:T(8,128)(2,1)}) %all-gather.20.cloned.1.call-update) | async-done | bytes 4194320 | tf_op jit(solution)/shard_map/all_gather | solution.py:35
  383.4 20.9 %while.59 = (s32[]{:T(128)}, f32[16,128,128]{2,1,0:T(8,128)}, s32[]{:T(128)}, bf16[8,16]{1,0:T(8,128)(2,1)S(1)}, bf16[8,16,128,128]{3,2,1,0:T(8,128)(2,1)}, /*index=5*/s32[]{:T(128)}, s32[]{:T(128)}, s32[]{:T(128)}, s32[]{:T(128)}) while((s32[]{:T(128)}, f32[16,128,128]{2,1,0:T(8,128)}, s32[]{:T(128)}, ...), condition=%wide.region_10.11_spmd.clone, body=%wide.region_9.10_spmd.clone.sunk | while | flops 1310744 | bytes 2621775 | solution.py:53
  420.3 3.6 multiply_reduce_fusion.3
  423.9 8.1 %multiply_bitcast_fusion = f32[2048,2048]{0,1:T(8,128)} fusion(bf16[128,2048]{1,0:T(8,128)(2,1)S(1)} %get-tuple-element.476, bf16[1,128,2048]{2,1,0:T(8,128)(2,1)S(1)} %copy-done), kind=kOutput, calls=%fused_computation.10 | convolution fusion | flops 1077936128 | bytes 17825792 | tf_op jit(solution)/shard_map/dot_general | solution.py:262
  438.3 4.3 multiply_reduce_fusion.7
  445.1 8.5 %fusion.2 = bf16[1,128,2048]{2,1,0:T(8,128)(2,1)} fusion(bf16[128,2048]{1,0:T(8,128)(2,1)S(1)} %get-tuple-element.476, bf16[2048,2048]{1,0:T(8,128)(2,1)} %all-gather.12.cloned.1.call-done), kind=kOutput, calls=%fused_computation.13 | convolution fusion | flops 1074003968 | bytes 9437184 | tf_op jit(solution)/shard_map/dot_general | solution.py:251
  453.6 156.4 %reduce-scatter.2.cloned.1.call-done = f32[128,2048]{0,1:T(8,128)} async-done(((f32[2048,2048]{0,1:T(8,128)}), f32[128,2048]{0,1:T(8,128)}) %reduce-scatter.2.cloned.1.call-update) | async-done | bytes 1048592 | tf_op jit(solution)/shard_map/reduce_scatter | solution.py:261
  612.5 89.3 %all-reduce.4.cloned.1.call-done = f32[3,4,2048]{2,1,0:T(4,128)} async-done(((f32[3,4,2048]{2,1,0:T(4,128)}), f32[3,4,2048]{2,1,0:T(4,128)}) %all-reduce.4.cloned.1.call-update) | async-done | bytes 98320 | tf_op jit(solution)/shard_map/psum | solution.py:250
  (176 shorter events, 120.1 us)
Async XLA Ops:
  7.2 80.1 %copy-start = (bf16[1,128,2048]{2,1,0:T(8,128)(2,1)S(1)}, bf16[1,128,2048]{2,1,0:T(8,128)(2,1)}, u32[]{:S(2)}) copy-start(bf16[1,128,2048]{2,1,0:T(8,128)(2,1)} %param.15) | copy-start | bytes 1572868
  7.2 80.1 %all-gather.12.cloned.1.call-start = ((), (), s32[]{:S(2)}) async-start(), calls=%async_computation.1 | async-start | bytes 8912896 | tf_op jit(solution)/shard_map/all_gather | solution.py:107
  7.9 174.5 %all-gather.14.cloned.1.call-start = ((), (), s32[]{:S(2)}) async-start(), calls=%async_computation.4 | async-start | bytes 9437184 | tf_op jit(solution)/shard_map/all_gather | solution.py:20
  11.9 83.1 %copy-start.22 = (bf16[1,128,2048]{2,1,0:T(8,128)(2,1)S(1)}, bf16[1,128,2048]{2,1,0:T(8,128)(2,1)}, u32[]{:S(2)}) copy-start(bf16[1,128,2048]{2,1,0:T(8,128)(2,1)} %param.18) | copy-start | bytes 1572868
  92.0 3.0 collective-permute-start
  99.2 165.5 %all-gather.16.cloned.1.call-start = ((), (), s32[]{:S(2)}) async-start(), calls=%async_computation.5 | async-start | bytes 9437184 | tf_op jit(solution)/shard_map/all_gather | solution.py:20
  101.5 2.4 copy-start.24
  101.5 20.2 %copy-start.23 = (bf16[1,128,2048]{2,1,0:T(8,128)(2,1)S(1)}, bf16[1,128,2048]{2,1,0:T(8,128)(2,1)}, u32[]{:S(2)}) copy-start(bf16[1,128,2048]{2,1,0:T(8,128)(2,1)} %param.17) | copy-start | bytes 1572868
  101.6 234.7 %all-gather.18.cloned.1.call-start = ((), (), s32[]{:S(2)}) async-start(), calls=%async_computation.6 | async-start | bytes 4718592 | tf_op jit(solution)/shard_map/all_gather | solution.py:35
  284.4 2.0 copy-start.10
  284.4 2.0 copy-start.20
  290.9 92.4 %all-gather.20.cloned.1.call-start = ((), (), s32[]{:S(2)}) async-start(), calls=%async_computation.7 | async-start | bytes 4718592 | tf_op jit(solution)/shard_map/all_gather | solution.py:35
  293.3 316.7 %reduce-scatter.2.cloned.1.call-start = ((), (), s32[]{:S(2)}) async-start(), calls=%async_computation.2 | async-start | bytes 17825792 | tf_op jit(solution)/shard_map/reduce_scatter | solution.py:261
  356.4 2.8 copy-start.5
  356.4 2.8 copy-start.11
  404.2 2.1 copy-start.8
  404.2 2.2 copy-start.21
  409.9 2.2 copy-start.18
  413.5 2.1 copy-start.19
  416.4 3.9 collective-permute-start.1
  432.0 2.4 copy-start.15
  432.0 269.8 %all-reduce.4.cloned.1.call-start = ((), (), s32[]{:S(2)}) async-start(), calls=%async_computation.3 | async-start | bytes 196608 | tf_op jit(solution)/shard_map/psum | solution.py:250
  438.3 4.3 copy-start.2
  438.3 4.3 copy-start.16
  (10 other events, 14.2 us)
Sparse Core Ops, SparseCore 0:
  10.2 76.9 all-gather.11
  99.3 83.1 all-gather.13
  184.1 80.5 all-gather.15
  291.1 45.1 all-gather.17
  337.7 45.6 all-gather.19
  432.1 177.8 reduce-scatter.1
  614.0 87.7 all-reduce.3
where the time goes:
time: 712 us; the launch traced here: 710 us
  waiting for transfers between devices  498 us (70%)
  other arithmetic  75.9 us (11%)
  matrix products  51.7 us (7%)
  local copies, waits for them, and re-layouts  34.8 us (5%)
  blocking collectives  30.8 us (4%)
  between operations  15.2 us (2%)
    reduce_scatter x1, waiting for transfers between devices, local(): lax.psum_scatter(lax.dot_general(columns, grad_value, (((0,), (0,)), ((),...  156 us
    all_gather x2, waiting for transfers between devices, prefix(): gathered = jax.tree.map(lambda a: lax.all_gather(a, axis), part)  133 us
    psum x1, waiting for transfers between devices, local(): grad_conv = lax.psum(kernel_terms, ('seq', 'rep'))  89.3 us
    all_gather x1, waiting for transfers between devices, local(): lax.all_gather(value_weight, ('seq', 'rep'), axis=0, tiled=True)  75.4 us
    all_gather x2, waiting for transfers between devices, carried_in(): lax.all_gather(part.astype(kind), axis)  42.3 us
    select_n x16, other arithmetic, step(): return jax.tree.map(lambda a, b: jnp.where(reached, a, b), new, before)  40.9 us
    unnamed x2, blocking collectives  30.8 us
    add x7, other arithmetic, chain_join(): following[0][:, None, None] * earlier[1] + following[1]  18.6 us
  transfers between devices with their start and end apart: 9, of which 8 were waited for; matrix products, arithmetic and copies ran while one was open for 11% of the time, Pallas kernels for 0%

commit v1 on v0

--- a/solution.py
+++ b/solution.py
@@ -91,6 +91,13 @@
 
 
 def local(activations, value_weight, query_in, key_in, grad_out, conv_kernel, log_gate):
+
+    def stacks_all_convert(x_part, axis_name):
+        return jnp.concatenate(
+            lax.all_to_all(jnp.stack(lax.axis_size(axis_name) * [x_part], 0), axis_name, 0, 0),
+            axis=0,
+        )
+
     tok_rows = query_in.shape[1]
     channels = query_in.shape[2]
     head_count = log_gate.shape[1]
@@ -104,7 +111,7 @@
     columns = gathered
     value_f32 = jnp.dot(
         columns,
-        lax.all_gather(value_weight, ("seq", "rep"), axis=0, tiled=True),
+        stacks_all_convert(value_weight, ("seq", "rep")),
         preferred_element_type=jnp.float32,
     )
     value_raw = value_f32.astype(jnp.bfloat16)

time: 712 us -> 858 us (1.21)
  waiting for transfers between devices: 498 us -> 601 us
  blocking collectives: 30.8 us -> 52.5 us
  starting transfers between devices: 3.96 us -> 22.3 us
    all_to_all x0 -> x1, waiting for transfers between devices: none -> 150 us  [stacks_all_convert(): lax.all_to_all(jnp.stack(lax.axis_size(axis_name) * [x_part], 0), axis_na...]
    all_gather x1, waiting for transfers between devices: 75.4 us -> 11.6 us  [local(): lax.all_gather(value_weight, ('seq', 'rep'), axis=0, tiled=True)]
    unnamed x2, blocking collectives: 30.8 us -> 52.5 us
    reduce_scatter x1, waiting for transfers between devices: 156 us -> 173 us  [local(): lax.psum_scatter(lax.dot_general(columns, grad_value, (((0,), (0,)), ((),...]
    ppermute x2, starting transfers between devices: 3.45 us -> 14.3 us  [shifted(): return lax.ppermute(block, axis, route)]
  transfers between devices with their start and end apart: 9 -> 10, of which waited for: 8 -> 9; matrix products, arithmetic and copies ran while one was open for 11% -> 14% of each run, Pallas kernels for 0% -> 0%
where the time goes in v1:
time: 858 us; the launch traced here: 856 us
  waiting for transfers between devices  601 us (70%)
  other arithmetic  76.1 us (9%)
  blocking collectives  52.5 us (6%)
  matrix products  48.6 us (6%)
  local copies, waits for them, and re-layouts  40.7 us (5%)
  starting transfers between devices  22.3 us (3%)
  between operations  15.2 us (2%)
    reduce_scatter x1, waiting for transfers between devices, local(): lax.psum_scatter(lax.dot_general(columns, grad_value, (((0,), (0,)), ((),...  173 us
    all_to_all x1, waiting for transfers between devices, stacks_all_convert(): lax.all_to_all(jnp.stack(lax.axis_size(axis_name) * [x_part], 0), axis_na...  150 us
    all_gather x2, waiting for transfers between devices, prefix(): gathered = jax.tree.map(lambda a: lax.all_gather(a, axis), part)  132 us
    psum x1, waiting for transfers between devices, local(): grad_conv = lax.psum(kernel_terms, ('seq', 'rep'))  89.3 us
    unnamed x2, blocking collectives  52.5 us
    all_gather x2, waiting for transfers between devices, carried_in(): lax.all_gather(part.astype(kind), axis)  43.4 us
    select_n x16, other arithmetic, step(): return jax.tree.map(lambda a, b: jnp.where(reached, a, b), new, before)  40.7 us
    add x7, other arithmetic, chain_join(): following[0][:, None, None] * earlier[1] + following[1]  18.8 us
  transfers between devices with their start and end apart: 10, of which 9 were waited for; matrix products, arithmetic and copies ran while one was open for 14% of the time, Pallas kernels for 0%

profile of v1, /device:TPU:0, one launch (start us, length us, event | category | flops | bytes accessed | tf_op | source)
XLA Modules:
  0.0 856.3 jit_solution(6613501942638528276)
XLA Ops:
  7.2 5.4 stack.88
  12.6 7.6 all-to-all-start
  21.6 150.2 %all-to-all-done = bf16[16,128,2048]{2,1,0:T(8,128)(2,1)} async-done(((bf16[16,128,2048]{2,1,0:T(8,128)(2,1)}), bf16[16,128,2048]{2,1,0:T(8,128)(2,1)}, u32[]{:S(2)}, u32[]{:S(2)}) %all-to-all-start) | async-done | bytes 8388640 | tf_op jit(solution)/shard_map/all_to_all | solution.py:97
  171.8 4.6 convolution_convert_fusion.1
  176.5 13.0 %collective-permute-start = (bf16[3,3,2048]{2,1,0:T(4,128)(2,1)S(1)}, bf16[3,3,2048]{2,1,0:T(4,128)(2,1)S(1)}, u32[]{:S(2)}, u32[]{:S(2)}) collective-permute-start(bf16[3,3,2048]{2,1,0:T(4,128)(2,1)S(1)} %pad_maximum_fusion.5), channel_id=1, source_target_pairs={{0,2},{2,4},{4,6},{6,8},{8,10},{10,12},{12,14},{1,3},{3,5},{5,7},{... | collective-permute-start | bytes 110600 | tf_op jit(solution)/shard_map/ppermute | solution.py:13
  199.9 38.0 %all-reduce = f32[128]{0:T(128)S(1)} all-reduce(f32[128]{0:T(128)S(1)} %dynamic-update-slice), channel_id=2, replica_groups=mesh['parts'=2,'seq'=8,'rep'=2,'head'=1] {'seq'}, use_global_device_ids=true, to_apply=%add | all-reduce | flops 128 | bytes 1024
  246.4 53.7 %all-gather.14.cloned.1.call-done = f32[128,128,128]{2,1,0:T(8,128)} async-done(((f32[16,128,128]{2,1,0:T(8,128)}), f32[128,128,128]{2,1,0:T(8,128)}) %all-gather.14.cloned.1.call-update) | async-done | bytes 8388624 | tf_op jit(solution)/shard_map/all_gather | solution.py:20
  303.8 78.4 %all-gather.16.cloned.1.call-done = f32[128,128,128]{2,1,0:T(8,128)} async-done(((f32[16,128,128]{2,1,0:T(8,128)}), f32[128,128,128]{2,1,0:T(8,128)}) %all-gather.16.cloned.1.call-update) | async-done | bytes 8388624 | tf_op jit(solution)/shard_map/all_gather | solution.py:20
  383.3 18.8 %while.57 = (s32[]{:T(128)}, f32[16,128,128]{2,1,0:T(8,128)}, s32[]{:T(128)}, f32[8,16]{1,0:T(8,128)S(1)}, f32[8,16,128,128]{3,2,1,0:T(8,128)}, /*index=5*/s32[]{:T(128)}, s32[]{:T(128)}, s32[]{:T(128)}, s32[]{:T(128)}) while((s32[]{:T(128)}, f32[16,128,128]{2,1,0:T(8,128)}, s32[]{:T(128)}, f32[8,16]{1,0:T(8,128)S(1)}, ...), condition=%wide.region_4.5_spmd, body=%wide.region_3.4_spmd.sunk | while | flops 524294 | bytes 3146067 | solution.py:29
  383.3 2.7 bitcast_add_fusion.5
  412.1 14.6 %all-reduce.1 = bf16[128]{0:T(256)(128)(2,1)S(1)} all-reduce(bf16[128]{0:T(256)(128)(2,1)S(1)} %dynamic-update-slice.1), channel_id=7, replica_groups=mesh['parts'=2,'seq'=8,'rep'=2,'head'=1] {'seq'}, use_global_device_ids=true, to_apply=%add.1 | all-reduce | flops 128 | bytes 512
  434.9 19.0 %all-gather.18.cloned.1.call-done = bf16[128,128,128]{2,1,0:T(8,128)(2,1)} async-done(((bf16[16,128,128]{2,1,0:T(8,128)(2,1)}), bf16[128,128,128]{2,1,0:T(8,128)(2,1)}) %all-gather.18.cloned.1.call-update) | async-done | bytes 4194320 | tf_op jit(solution)/shard_map/all_gather | solution.py:35
  453.9 20.0 %while.58 = (s32[]{:T(128)}, f32[16,128,128]{2,1,0:T(8,128)}, s32[]{:T(128)}, bf16[8,16]{1,0:T(8,128)(2,1)S(1)}, bf16[8,16,128,128]{3,2,1,0:T(8,128)(2,1)}, /*index=5*/s32[]{:T(128)}, s32[]{:T(128)}) while((s32[]{:T(128)}, f32[16,128,128]{2,1,0:T(8,128)}, s32[]{:T(128)}, bf16[8,16]{1,0:T(8,128)(2,1)S(1)}, ...), condition=%wide.region_8.9_spmd.clone, body=%wide.region_7.8_spmd.clone.sunk | while | flops 1310740 | bytes 2621705 | solution.py:53
  474.0 2.8 fusion.10
  476.8 24.4 %all-gather.20.cloned.1.call-done = bf16[128,128,128]{2,1,0:T(8,128)(2,1)} async-done(((bf16[16,128,128]{2,1,0:T(8,128)(2,1)}), bf16[128,128,128]{2,1,0:T(8,128)(2,1)}) %all-gather.20.cloned.1.call-update) | async-done | bytes 4194320 | tf_op jit(solution)/shard_map/all_gather | solution.py:35
  501.2 20.8 %while.59 = (s32[]{:T(128)}, f32[16,128,128]{2,1,0:T(8,128)}, s32[]{:T(128)}, bf16[8,16]{1,0:T(8,128)(2,1)S(1)}, bf16[8,16,128,128]{3,2,1,0:T(8,128)(2,1)}, /*index=5*/s32[]{:T(128)}, s32[]{:T(128)}, s32[]{:T(128)}, s32[]{:T(128)}) while((s32[]{:T(128)}, f32[16,128,128]{2,1,0:T(8,128)}, s32[]{:T(128)}, ...), condition=%wide.region_10.11_spmd.clone, body=%wide.region_9.10_spmd.clone.sunk | while | flops 1310744 | bytes 2621767 | solution.py:53
  508.7 2.7 fusion.120
  538.9 3.8 multiply_reduce_fusion.3
  542.7 8.1 multiply_bitcast_fusion
  558.0 4.1 multiply_reduce_fusion.11
  564.7 11.6 %all-gather.12.cloned.1.call-done = bf16[2048,2048]{1,0:T(8,128)(2,1)} async-done(((bf16[128,2048]{1,0:T(8,128)(2,1)}), bf16[2048,2048]{1,0:T(8,128)(2,1)}) %all-gather.12.cloned.1.call-update) | async-done | bytes 8388624 | tf_op jit(solution)/shard_map/all_gather | solution.py:260
  576.3 7.1 fusion.2
  583.4 172.6 %reduce-scatter.2.cloned.1.call-done = f32[128,2048]{0,1:T(8,128)} async-done(((f32[2048,2048]{0,1:T(8,128)}), f32[128,2048]{0,1:T(8,128)}) %reduce-scatter.2.cloned.1.call-update) | async-done | bytes 1048592 | tf_op jit(solution)/shard_map/reduce_scatter | solution.py:268
  758.6 89.3 %all-reduce.4.cloned.1.call-done = f32[3,4,2048]{2,1,0:T(4,128)} async-done(((f32[3,4,2048]{2,1,0:T(4,128)}), f32[3,4,2048]{2,1,0:T(4,128)}) %all-reduce.4.cloned.1.call-update) | async-done | bytes 98320 | tf_op jit(solution)/shard_map/psum | solution.py:257
  (183 shorter events, 127.3 us)
Async XLA Ops:
  7.2 164.7 %copy-start = (bf16[1,128,2048]{2,1,0:T(8,128)(2,1)S(1)}, bf16[1,128,2048]{2,1,0:T(8,128)(2,1)}, u32[]{:S(2)}) copy-start(bf16[1,128,2048]{2,1,0:T(8,128)(2,1)} %param.15) | copy-start | bytes 1572868
  12.6 8.4 copy-start.22
  12.6 8.4 copy-start.25
  12.6 8.9 %copy-start.24 = (f32[3,4,2048]{2,1,0:T(4,128)S(1)}, f32[3,4,2048]{2,1,0:T(4,128)}, u32[]{:S(2)}) copy-start(f32[3,4,2048]{2,1,0:T(4,128)} %param.20) | copy-start | bytes 294916
  12.6 159.2 %all-to-all-start = ((bf16[16,128,2048]{2,1,0:T(8,128)(2,1)}), bf16[16,128,2048]{2,1,0:T(8,128)(2,1)}, u32[]{:S(2)}, u32[]{:S(2)}) async-start(bf16[16,128,2048]{2,1,0:T(8,128)(2,1)} %stack.88), calls=%async_computation | async-start | bytes 16777216 | tf_op jit(solution)/shard_map/all_to_all | solution.py:97
  20.1 280.0 %all-gather.14.cloned.1.call-start = ((), (), s32[]{:S(2)}) async-start(), calls=%async_computation.5 | async-start | bytes 9437184 | tf_op jit(solution)/shard_map/all_gather | solution.py:20
  176.5 13.8 %collective-permute-start = (bf16[3,3,2048]{2,1,0:T(4,128)(2,1)S(1)}, bf16[3,3,2048]{2,1,0:T(4,128)(2,1)S(1)}, u32[]{:S(2)}, u32[]{:S(2)}) collective-permute-start(bf16[3,3,2048]{2,1,0:T(4,128)(2,1)S(1)} %pad_maximum_fusion.5), channel_id=1, source_target_pairs={{0,2},{2,4},{4,6},{6,8},{8,10},{10,12},{12,14},{1,3},{3,5},{5,7},{... | collective-permute-start | bytes 110600 | tf_op jit(solution)/shard_map/ppermute | solution.py:13
  193.3 2.7 copy-start.9
  195.9 186.2 %all-gather.16.cloned.1.call-start = ((), (), s32[]{:S(2)}) async-start(), calls=%async_computation.6 | async-start | bytes 9437184 | tf_op jit(solution)/shard_map/all_gather | solution.py:20
  196.0 2.4 copy-start.26
  198.3 41.9 %copy-start.23 = (bf16[1,128,2048]{2,1,0:T(8,128)(2,1)S(1)}, bf16[1,128,2048]{2,1,0:T(8,128)(2,1)}, u32[]{:S(2)}) copy-start(bf16[1,128,2048]{2,1,0:T(8,128)(2,1)} %param.17) | copy-start | bytes 1572868
  198.3 255.6 %all-gather.18.cloned.1.call-start = ((), (), s32[]{:S(2)}) async-start(), calls=%async_computation.7 | async-start | bytes 4718592 | tf_op jit(solution)/shard_map/all_gather | solution.py:35
  402.1 2.0 copy-start.13
  402.1 2.0 copy-start.20
  408.7 92.5 %all-gather.20.cloned.1.call-start = ((), (), s32[]{:S(2)}) async-start(), calls=%async_computation.8 | async-start | bytes 4718592 | tf_op jit(solution)/shard_map/all_gather | solution.py:35
  411.0 165.3 %all-gather.12.cloned.1.call-start = ((), (), s32[]{:S(2)}) async-start(), calls=%async_computation.2 | async-start | bytes 8912896 | tf_op jit(solution)/shard_map/all_gather | solution.py:260
  411.6 344.4 %reduce-scatter.2.cloned.1.call-start = ((), (), s32[]{:S(2)}) async-start(), calls=%async_computation.3 | async-start | bytes 17825792 | tf_op jit(solution)/shard_map/reduce_scatter | solution.py:268
  521.9 2.3 copy-start.18
  525.6 2.1 copy-start.11
  532.0 2.1 copy-start.19
  534.9 3.9 collective-permute-start.1
  550.8 297.1 %all-reduce.4.cloned.1.call-start = ((), (), s32[]{:S(2)}) async-start(), calls=%async_computation.4 | async-start | bytes 196608 | tf_op jit(solution)/shard_map/psum | solution.py:257
  555.4 2.7 copy-start.2
  558.0 4.1 copy-start.16
  (13 other events, 17.1 us)
Sparse Core Ops, SparseCore 0:
  196.0 104.0 all-gather.13
  301.7 80.4 all-gather.15
  408.8 45.1 all-gather.17
  455.4 45.7 all-gather.19
  503.2 73.0 all-gather.11
  580.3 175.6 reduce-scatter.1
  760.0 87.8 all-reduce.3
